TPU v7x, 32 devices: a whole 2x2x4 slice. The times are simulated.
32 devices in a mesh: fsdp: 8 (over z, y), ctx: 2 (over x), tp: 2 (over core).
Axes of the slice: x: 2, y: 2, z: 4, core: 2. Of those that a mesh axis runs over, the one named last changes fastest.
Arguments:
- tokens_in: bfloat16 [4096, 2048], P(('fsdp', 'ctx')), may hold values from -6 to 6
- doc_positions: int32 [4096], P(('fsdp', 'ctx')), may hold values from 0 to 383, as said below
- attn_gain: bfloat16 [2048], P('fsdp'), may hold values from 0.25 to 1.75
- query_weight: bfloat16 [2048, 2048], P('fsdp', 'tp'), may hold values from -1 to 1
- key_weight: bfloat16 [2048, 256], P('fsdp', 'tp'), may hold values from -1 to 1
- value_weight: bfloat16 [2048, 256], P('fsdp', 'tp'), may hold values from -0.125 to 0.125
- output_weight: bfloat16 [2048, 2048], P('fsdp', 'tp'), may hold values from -2 to 2
- mlp_gain: bfloat16 [2048], P('fsdp'), may hold values from 0.25 to 1.75
- gate_weight: bfloat16 [2048, 5632], P('fsdp', 'tp'), may hold values from -0.125 to 0.125
- up_weight: bfloat16 [2048, 5632], P('fsdp', 'tp'), may hold values from -0.125 to 0.125
- down_weight: bfloat16 [2048, 5632], P('fsdp', 'tp'), may hold values from -0.078125 to 0.078125
- cotangent: bfloat16 [4096, 2048], P(('fsdp', 'ctx')), may hold values from -6 to 6
Outputs:
- block_out: bfloat16 [4096, 2048], P(('fsdp', 'ctx'))
- grad_tokens: float32 [4096, 2048], P(('fsdp', 'ctx'))
- grad_attn_gain: float32 [2048], P('fsdp')
- grad_query: float32 [2048, 2048], P('fsdp', 'tp')
- grad_key: float32 [2048, 256], P('fsdp', 'tp')
- grad_value: float32 [2048, 256], P('fsdp', 'tp')
- grad_output: float32 [2048, 2048], P('fsdp', 'tp')
- grad_mlp_gain: float32 [2048], P('fsdp')
- grad_gate: float32 [2048, 5632], P('fsdp', 'tp')
- grad_up: float32 [2048, 5632], P('fsdp', 'tp')
- grad_down: float32 [2048, 5632], P('fsdp', 'tp')
Inputs may be any that keep to these rules, and one draw needn't show every extreme that they name: `doc_positions`: each sequence of 512 tokens is packed with documents and begins with a new one; a token's value is its offset within its document: 0 at a document's first token, rising by one along it. Documents hold 102 to 384 tokens, except that the last of a sequence may be cut short; some document holds exactly 384.
All inputs are finite; a program needn't handle non-finite values.
Results may differ from a plain program's by a relative error of at most 0.014.
The roundings to bfloat16 on the way count: a program that leaves them out, or rounds other values in their place, can miss the bound.
Values may be sent and summed in bfloat16 or wider, within the bound.
No kernel may reach another device: no remote copies, remote signals or barrier semaphores. Data moves between devices by JAX's collectives and lax.ppermute only.
A program may use at most 256 MiB of HBM per device.

v0:
```python
import jax
import jax.numpy as jnp
from jax import lax
from jax.sharding import PartitionSpec as P

HEADS = 32
KV_HEADS = 4
HEAD_DIM = 64
EPSILON = 1e-05
NEG_FILL = -1e30


def rotary_tables(positions):
    half_dim = HEAD_DIM // 2
    inverse = 1.0 / 10000.0 ** (jnp.arange(half_dim, dtype=jnp.float32) * (2.0 / HEAD_DIM))
    angles = positions.astype(jnp.float32)[:, None] * inverse[None, :]
    cosine_table = jnp.concatenate([jnp.cos(angles), jnp.cos(angles)], axis=-1)[:, None, :]
    sine_table = jnp.concatenate([jnp.sin(angles), jnp.sin(angles)], axis=-1)[:, None, :]
    return (cosine_table, sine_table)


def apply_rotary(values, cosine_table, sine_table):
    half_dim = values.shape[-1] // 2
    turned = jnp.concatenate([-values[..., half_dim:], values[..., :half_dim]], axis=-1)
    return values * cosine_table + turned * sine_table


def undo_rotary(gradient, cosine_table, sine_table):
    half_dim = gradient.shape[-1] // 2
    sined = gradient * sine_table
    return gradient * cosine_table + jnp.concatenate(
        [sined[..., half_dim:], -sined[..., :half_dim]], axis=-1
    )


def contract_last(left_array, right_array):
    return lax.dot_general(
        left_array, right_array, (((1,), (1,)), ((), ())), preferred_element_type=jnp.float32
    )


def contract_first(left_array, right_array):
    return lax.dot_general(
        left_array, right_array, (((0,), (0,)), ((), ())), preferred_element_type=jnp.float32
    )


def normed_fold(scaled, pieces):
    gain_float = pieces[0].astype(jnp.float32)
    normed = (scaled * gain_float[None, :]).astype(jnp.bfloat16)
    sums = tuple(
        (jnp.dot(normed, matrix, preferred_element_type=jnp.float32) for matrix in pieces[1:])
    )
    return sums + (normed, gain_float)


def row_fold(left_array, shard_piece):
    return jnp.dot(left_array, shard_piece, preferred_element_type=jnp.float32)


def column_fold(gradients_in, pieces):
    part_sum = contract_last(gradients_in[0], pieces[0])
    for grad_piece, weight_piece in zip(gradients_in[1:], pieces[1:]):
        part_sum = part_sum + contract_last(grad_piece, weight_piece)
    return part_sum


def column_map(left_array, shard_piece):
    return contract_last(left_array, shard_piece)


def tensor_total(partial_sum):
    return lax.psum(partial_sum, "tp")


def body(
    tokens_in,
    doc_positions,
    attn_gain,
    query_weight,
    key_weight,
    value_weight,
    output_weight,
    mlp_gain,
    gate_weight,
    up_weight,
    down_weight,
    cotangent,
):
    local_rows = tokens_in.shape[0]
    query_columns = query_weight.shape[1]
    key_columns = key_weight.shape[1]
    local_groups = key_columns // HEAD_DIM
    group_size = HEADS // KV_HEADS
    group_width = group_size * HEAD_DIM
    score_scale = HEAD_DIM ** (-0.5)
    tokens = tokens_in.astype(jnp.float32)
    rms_one = lax.rsqrt(jnp.mean(tokens * tokens, axis=-1, keepdims=True) + EPSILON)
    scaled_one = tokens * rms_one
    query_lin, key_lin, value_lin, normed_one, gain_one = normed_fold(
        scaled_one,
        (
            lax.all_gather(attn_gain, "fsdp", axis=0, tiled=True),
            lax.all_gather(query_weight, "fsdp", axis=0, tiled=True),
            lax.all_gather(key_weight, "fsdp", axis=0, tiled=True),
            lax.all_gather(value_weight, "fsdp", axis=0, tiled=True),
        ),
    )
    cosine_table, sine_table = rotary_tables(doc_positions)
    queries = (
        apply_rotary(query_lin.reshape(local_rows, -1, HEAD_DIM), cosine_table, sine_table)
        .astype(jnp.bfloat16)
        .reshape(local_rows, query_columns)
    )
    keys_low = (
        apply_rotary(key_lin.reshape(local_rows, -1, HEAD_DIM), cosine_table, sine_table)
        .astype(jnp.bfloat16)
        .reshape(local_rows, key_columns)
    )
    values_low = value_lin.astype(jnp.bfloat16)
    key_all, value_all = (
        lax.all_gather(keys_low, "ctx", axis=0, tiled=True),
        lax.all_gather(values_low, "ctx", axis=0, tiled=True),
    )
    key_count = key_all.shape[0]
    query_places = lax.axis_index("ctx") * local_rows + jnp.arange(local_rows, dtype=jnp.int32)
    key_places = jnp.arange(key_count, dtype=jnp.int32)
    allowed = (key_places[None, :] <= query_places[:, None]) & (
        key_places[None, :] >= (query_places - doc_positions)[:, None]
    )

    def head_scores(query_group, key_head):
        raw_scores = (
            jnp.einsum("ngd,kd->gnk", query_group, key_head, preferred_element_type=jnp.float32)
            * score_scale
        )
        return jnp.where(allowed[None], raw_scores, NEG_FILL)

    attended_parts = []
    lse_parts = []
    for group_index in range(local_groups):
        query_group = queries[
            :, group_index * group_width : (group_index + 1) * group_width
        ].reshape(local_rows, group_size, HEAD_DIM)
        key_head = key_all[:, group_index * HEAD_DIM : (group_index + 1) * HEAD_DIM]
        value_head = value_all[:, group_index * HEAD_DIM : (group_index + 1) * HEAD_DIM]
        scores = head_scores(query_group, key_head)
        largest = jnp.max(scores, axis=-1, keepdims=True)
        exponent = jnp.exp(scores - largest)
        totals = jnp.sum(exponent, axis=-1, keepdims=True)
        probs_low = (exponent / totals).astype(jnp.bfloat16)
        attended_parts.append(
            jnp.einsum(
                "gnk,kd->ngd", probs_low, value_head, preferred_element_type=jnp.float32
            ).reshape(local_rows, group_width)
        )
        lse_parts.append(largest + jnp.log(totals))
    attended_low = jnp.concatenate(attended_parts, axis=1).astype(jnp.bfloat16)
    attn_branch = tensor_total(
        column_map(attended_low, lax.all_gather(output_weight, "fsdp", axis=0, tiled=True))
    )
    residual = tokens + attn_branch
    rms_two = lax.rsqrt(jnp.mean(residual * residual, axis=-1, keepdims=True) + EPSILON)
    scaled_two = residual * rms_two
    gate_lin, up_lin, normed_two, gain_two = normed_fold(
        scaled_two,
        (
            lax.all_gather(mlp_gain, "fsdp", axis=0, tiled=True),
            lax.all_gather(gate_weight, "fsdp", axis=0, tiled=True),
            lax.all_gather(up_weight, "fsdp", axis=0, tiled=True),
        ),
    )
    silu_value = gate_lin / (1.0 + jnp.exp(-gate_lin))
    act_low = (silu_value * up_lin).astype(jnp.bfloat16)
    mlp_branch = tensor_total(
        column_map(act_low, lax.all_gather(down_weight, "fsdp", axis=0, tiled=True))
    )
    block_out = (residual + mlp_branch).astype(jnp.bfloat16)
    grad_out = cotangent.astype(jnp.float32)
    grad_act = row_fold(cotangent, lax.all_gather(down_weight, "fsdp", axis=0, tiled=True))
    sigmoid = 1.0 / (1.0 + jnp.exp(-gate_lin))
    grad_gate_lin = (grad_act * up_lin * sigmoid * (1.0 + gate_lin * (1.0 - sigmoid))).astype(
        jnp.bfloat16
    )
    grad_up_lin = (grad_act * silu_value).astype(jnp.bfloat16)
    grad_normed_two = tensor_total(
        column_fold(
            (grad_gate_lin, grad_up_lin),
            (
                lax.all_gather(gate_weight, "fsdp", axis=0, tiled=True),
                lax.all_gather(up_weight, "fsdp", axis=0, tiled=True),
            ),
        )
    )
    scaled_grad_two = grad_normed_two * gain_two[None, :]
    grad_residual = (
        grad_out
        + rms_two * scaled_grad_two
        - residual
        * (rms_two * rms_two * rms_two)
        * jnp.mean(scaled_grad_two * residual, axis=-1, keepdims=True)
    )
    grad_attn_low = grad_residual.astype(jnp.bfloat16)
    grad_attended = row_fold(
        grad_attn_low, lax.all_gather(output_weight, "fsdp", axis=0, tiled=True)
    ).astype(jnp.bfloat16)
    query_grads = []
    key_grads = []
    value_grads = []
    for group_index in range(local_groups):
        query_group = queries[
            :, group_index * group_width : (group_index + 1) * group_width
        ].reshape(local_rows, group_size, HEAD_DIM)
        key_head = key_all[:, group_index * HEAD_DIM : (group_index + 1) * HEAD_DIM]
        value_head = value_all[:, group_index * HEAD_DIM : (group_index + 1) * HEAD_DIM]
        probabilities = jnp.exp(head_scores(query_group, key_head) - lse_parts[group_index])
        probs_low = probabilities.astype(jnp.bfloat16)
        grad_group = grad_attended[
            :, group_index * group_width : (group_index + 1) * group_width
        ].reshape(local_rows, group_size, HEAD_DIM)
        grad_probs = jnp.einsum(
            "ngd,kd->gnk", grad_group, value_head, preferred_element_type=jnp.float32
        )
        row_dot = jnp.sum(probabilities * grad_probs, axis=-1, keepdims=True)
        grad_scores = (probabilities * (grad_probs - row_dot)).astype(jnp.bfloat16)
        query_grads.append(
            jnp.einsum("gnk,kd->ngd", grad_scores, key_head, preferred_element_type=jnp.float32)
            * score_scale
        )
        key_grads.append(
            jnp.einsum("gnk,ngd->kd", grad_scores, query_group, preferred_element_type=jnp.float32)
            * score_scale
        )
        value_grads.append(
            jnp.einsum("gnk,ngd->kd", probs_low, grad_group, preferred_element_type=jnp.float32)
        )
    key_grad_local, value_grad_local = (
        lax.psum_scatter(
            jnp.concatenate(key_grads, axis=1), "ctx", scatter_dimension=0, tiled=True
        ),
        lax.psum_scatter(
            jnp.concatenate(value_grads, axis=1), "ctx", scatter_dimension=0, tiled=True
        ),
    )
    grad_q_lin = (
        undo_rotary(jnp.concatenate(query_grads, axis=1), cosine_table, sine_table)
        .astype(jnp.bfloat16)
        .reshape(local_rows, query_columns)
    )
    grad_k_lin = (
        undo_rotary(key_grad_local.reshape(local_rows, -1, HEAD_DIM), cosine_table, sine_table)
        .astype(jnp.bfloat16)
        .reshape(local_rows, key_columns)
    )
    grad_v_lin = value_grad_local.astype(jnp.bfloat16)
    grad_normed_one = tensor_total(
        column_fold(
            (grad_q_lin, grad_k_lin, grad_v_lin),
            (
                lax.all_gather(query_weight, "fsdp", axis=0, tiled=True),
                lax.all_gather(key_weight, "fsdp", axis=0, tiled=True),
                lax.all_gather(value_weight, "fsdp", axis=0, tiled=True),
            ),
        )
    )
    scaled_grad_one = grad_normed_one * gain_one[None, :]
    grad_tokens = (
        grad_residual
        + rms_one * scaled_grad_one
        - tokens
        * (rms_one * rms_one * rms_one)
        * jnp.mean(scaled_grad_one * tokens, axis=-1, keepdims=True)
    )
    owned = lax.psum_scatter(
        (
            jnp.sum(grad_normed_one * scaled_one, axis=0),
            contract_first(normed_one, grad_q_lin),
            contract_first(normed_one, grad_k_lin),
            contract_first(normed_one, grad_v_lin),
            contract_first(grad_attn_low, attended_low),
            jnp.sum(grad_normed_two * scaled_two, axis=0),
            contract_first(normed_two, grad_gate_lin),
            contract_first(normed_two, grad_up_lin),
            contract_first(cotangent, act_low),
        ),
        "fsdp",
        scatter_dimension=0,
        tiled=True,
    )
    (
        gain_one_grad,
        query_grad,
        key_grad,
        value_grad,
        output_grad,
        gain_two_grad,
        gate_grad,
        up_grad,
        down_grad,
    ) = owned
    summed = lax.psum(
        (
            gain_one_grad,
            query_grad,
            key_grad,
            value_grad,
            output_grad,
            gain_two_grad,
            gate_grad,
            up_grad,
            down_grad,
        ),
        "ctx",
    )
    return (
        block_out,
        grad_tokens,
        summed[0],
        summed[1],
        summed[2],
        summed[3],
        summed[4],
        summed[5],
        summed[6],
        summed[7],
        summed[8],
    )


def solution(mesh):
    return jax.shard_map(
        body,
        mesh=mesh,
        in_specs=(
            P(("fsdp", "ctx"), None),
            P(("fsdp", "ctx")),
            P("fsdp"),
            P("fsdp", "tp"),
            P("fsdp", "tp"),
            P("fsdp", "tp"),
            P("fsdp", "tp"),
            P("fsdp"),
            P("fsdp", "tp"),
            P("fsdp", "tp"),
            P("fsdp", "tp"),
            P(("fsdp", "ctx"), None),
        ),
        out_specs=(
            P(("fsdp", "ctx"), None),
            P(("fsdp", "ctx"), None),
            P("fsdp"),
            P("fsdp", "tp"),
            P("fsdp", "tp"),
            P("fsdp", "tp"),
            P("fsdp", "tp"),
            P("fsdp"),
            P("fsdp", "tp"),
            P("fsdp", "tp"),
            P("fsdp", "tp"),
        ),
        check_vma=False,
    )
```

profile of v0, /device:TPU:0, one launch (start us, length us, event | category | flops | bytes accessed | tf_op | source)
XLA Modules:
  0.0 2660.1 jit_solution(7111655742602666391)
XLA Ops:
  9.4 22.6 all-gather
  33.0 1.5 fusion.19
  35.1 33.7 %all_gather.43 = bf16[2048,128]{1,0:T(8,128)(2,1)S(1)} all-gather(bf16[256,128]{1,0:T(8,128)(2,1)S(1)} %copy-done.46), channel_id=1, replica_groups=mesh['fsdp'=8,'ctx'=2,'tp'=2] {'fsdp'}, dimensions={0}, use_global_device_ids=true | all-gather | bytes 589824 | tf_op jit(solution)/shard_map/all_gather | solution.py:105
  70.0 5.0 all_gather.44
  75.1 32.7 %all_gather.41 = bf16[2048,128]{1,0:T(8,128)(2,1)S(1)} all-gather(bf16[256,128]{1,0:T(8,128)(2,1)S(1)} %copy-done.47), channel_id=1, replica_groups=mesh['fsdp'=8,'ctx'=2,'tp'=2] {'fsdp'}, dimensions={0}, use_global_device_ids=true | all-gather | bytes 589824 | tf_op jit(solution)/shard_map/all_gather | solution.py:106
  108.3 5.0 all_gather.42
  114.1 3.5 fusion.62
  117.6 1.3 copy.71
  121.3 2.5 copy.72
  123.8 1.4 add_convert_fusion.1
  131.4 39.2 %all-gather.10.cloned.1.call-done = bf16[2048,1024]{1,0:T(8,128)(2,1)} async-done(((bf16[256,1024]{1,0:T(8,128)(2,1)}), bf16[2048,1024]{1,0:T(8,128)(2,1)}) %all-gather.10.cloned.1.call-update) | async-done | bytes 4194320 | tf_op jit(solution)/shard_map/all_gather | solution.py:160
  170.7 4.8 fusion.44
  177.3 18.3 all-gather.1
  195.7 1.9 multiply_reduce_fusion.2
  200.0 162.1 %all-gather.14.cloned.1.call-done = bf16[2048,2816]{1,0:T(8,128)(2,1)} async-done(((bf16[256,2816]{1,0:T(8,128)(2,1)}), bf16[2048,2816]{1,0:T(8,128)(2,1)}) %all-gather.14.cloned.1.call-update) | async-done | bytes 11534352 | tf_op jit(solution)/shard_map/all_gather | solution.py:170
  362.1 9.3 fusion.74
  371.4 154.2 %all-gather.12.cloned.1.call-done = bf16[2048,2816]{1,0:T(8,128)(2,1)} async-done(((bf16[256,2816]{1,0:T(8,128)(2,1)}), bf16[2048,2816]{1,0:T(8,128)(2,1)}) %all-gather.12.cloned.1.call-update) | async-done | bytes 11534352 | tf_op jit(solution)/shard_map/all_gather | solution.py:169
  525.6 9.3 fusion.73
  534.9 154.2 %all-gather.16.cloned.1.call-done = bf16[2048,2816]{1,0:T(8,128)(2,1)} async-done(((bf16[256,2816]{1,0:T(8,128)(2,1)}), bf16[2048,2816]{1,0:T(8,128)(2,1)}) %all-gather.16.cloned.1.call-update) | async-done | bytes 11534352 | tf_op jit(solution)/shard_map/all_gather | solution.py:176
  689.2 11.1 multiply_convert_fusion
  700.3 7.1 fusion.76
  707.4 8.8 convolution_add_fusion.2
  716.2 1.3 log_add_fusion
  717.6 1.3 log_add_fusion.1
  718.9 16.9 all-reduce.13.cloned.1.call-done
  735.8 2.9 multiply_reduce_fusion
  739.3 1.6 copy-done.59
  740.9 1.3 convolution_convert_fusion
  743.1 1.8 copy.82
  744.9 3.8 fusion.34
  748.7 3.5 fusion
  752.2 1.8 copy.79
  754.0 3.1 fusion.31
  757.6 3.5 fusion.3
  761.9 4.4 fusion.2
  766.5 2.0 copy-done.10
  771.9 3.0 reduce-scatter.12.cloned.1.call-done
  774.9 2.5 fusion.51
  777.8 11.7 reduce-scatter.10.cloned.1.call-done
  791.4 1.6 fusion.58
  793.0 6.3 fusion.40
  800.2 2.2 fusion.27
  804.3 4.8 fusion.60
  809.2 12.6 convolution_bitcast_fusion
  821.8 12.6 fusion.79
  834.7 12.6 fusion.78
  847.5 9.4 fusion.75
  856.8 1.3 fusion.77
  859.2 1.8 convolution_add_fusion
  861.1 63.5 %reduce-scatter.16.cloned.1.call-done = f32[256,128]{1,0:T(8,128)} async-done(((f32[2048,128]{1,0:T(8,128)}), f32[256,128]{1,0:T(8,128)}) %reduce-scatter.16.cloned.1.call-update) | async-done | bytes 131088 | tf_op jit(solution)/shard_map/reduce_scatter | solution.py:274
  924.6 149.9 %reduce-scatter.20.cloned.1.call-done = f32[256,1024]{1,0:T(8,128)} async-done(((f32[2048,1024]{1,0:T(8,128)}), f32[256,1024]{1,0:T(8,128)}) %reduce-scatter.20.cloned.1.call-update) | async-done | bytes 1048592 | tf_op jit(solution)/shard_map/reduce_scatter | solution.py:274
  1074.5 150.2 %reduce-scatter.14.cloned.1.call-done = f32[256,1024]{1,0:T(8,128)} async-done(((f32[2048,1024]{1,0:T(8,128)}), f32[256,1024]{1,0:T(8,128)}) %reduce-scatter.14.cloned.1.call-update) | async-done | bytes 1048592 | tf_op jit(solution)/shard_map/reduce_scatter | solution.py:274
  1224.8 376.5 %reduce-scatter.26.cloned.1.call-done = f32[256,2816]{0,1:T(8,128)} async-done(((f32[2048,2816]{0,1:T(8,128)}), f32[256,2816]{0,1:T(8,128)}) %reduce-scatter.26.cloned.1.call-update) | async-done | bytes 2883600 | tf_op jit(solution)/shard_map/reduce_scatter | solution.py:274
  1601.3 375.6 %reduce-scatter.24.cloned.1.call-done = f32[256,2816]{1,0:T(8,128)} async-done(((f32[2048,2816]{1,0:T(8,128)}), f32[256,2816]{1,0:T(8,128)}) %reduce-scatter.24.cloned.1.call-update) | async-done | bytes 2883600 | tf_op jit(solution)/shard_map/reduce_scatter | solution.py:274
  1976.9 375.6 %reduce-scatter.22.cloned.1.call-done = f32[256,2816]{1,0:T(8,128)} async-done(((f32[2048,2816]{1,0:T(8,128)}), f32[256,2816]{1,0:T(8,128)}) %reduce-scatter.22.cloned.1.call-update) | async-done | bytes 2883600 | tf_op jit(solution)/shard_map/reduce_scatter | solution.py:274
  2354.5 28.6 %all-reduce.15.cloned.1.call-done = (f32[256,2048]{1,0:T(8,128)}, f32[256,2048]{1,0:T(8,128)}) async-done(((f32[256,2048]{1,0:T(8,128)}, f32[256,2048]{1,0:T(8,128)}), (f32[256,2048]{1,0:T(8,128)}, f32[256,2048]{1,0:T(8,128)})) %all-reduce.15.cloned.1.call-update) | async-done | bytes 4194320 | tf_op jit(solution)/shard_map/psum | solution.py:73
  2383.1 2.3 fusion.14
  2385.3 37.3 %all-reduce.2 = (f32[2048]{0:T(1024)S(1)}, f32[2048]{0:T(1024)S(1)}) all-reduce(f32[2048]{0:T(1024)S(1)} %get-tuple-element.46, f32[2048]{0:T(1024)S(1)} %copy-done.52), channel_id=4, replica_groups=mesh['fsdp'=8,'ctx'=2,'tp'=2] {'fsdp'}, use_global_device_ids=true, to_apply=%region_17.18.clone | all-reduce | flops 4096 | bytes 32768
  2422.8 5.7 all-reduce.4
  2428.5 5.1 fusion.21
  2433.6 208.2 %all-reduce.17.cloned.1.call-done = (f32[256,1024]{1,0:T(8,128)}, f32[256,128]{1,0:T(8,128)}, f32[256,128]{1,0:T(8,128)}, f32[256,1024]{1,0:T(8,128)}, f32[256,2...) async-done(((f32[256,1024]{1,0:T(8,128)}, f32[256,128]{1,0:T(8,128)}, f32[256,128]{1,0:T(8,128)}, f32[256,1024]{1,0:T(8,128)}, f32[256,2816]{1,0:T(8,128)}, ...) | async-done | bytes 11010064 | tf_op jit(solution)/shard_map/psum | solution.py:301
  2641.9 3.5 copy.89
  2648.6 1.6 copy.121
  2651.5 1.6 copy.122
  (219 shorter events, 37.4 us)
Async XLA Ops:
  7.2 61.7 %copy-start.5 = (bf16[256,2048]{1,0:T(8,128)(2,1)S(1)}, bf16[256,2048]{1,0:T(8,128)(2,1)}, u32[]{:S(2)}) copy-start(bf16[256,2048]{1,0:T(8,128)(2,1)} %param.12) | copy-start | bytes 3145732
  7.2 28.0 %copy-start.46 = (bf16[256,128]{1,0:T(8,128)(2,1)S(1)}, bf16[256,128]{1,0:T(8,128)(2,1)}, u32[]{:S(2)}) copy-start(bf16[256,128]{1,0:T(8,128)(2,1)} %param.16) | copy-start | bytes 196612
  7.2 106.9 %all-gather.8.cloned.1.call-start = ((), (), s32[]{:S(2)}) async-start(), calls=%async_computation.9 | async-start | bytes 4718592 | tf_op jit(solution)/shard_map/all_gather | solution.py:104
  7.9 162.7 %all-gather.10.cloned.1.call-start = ((), (), s32[]{:S(2)}) async-start(), calls=%async_computation.10 | async-start | bytes 4718592 | tf_op jit(solution)/shard_map/all_gather | solution.py:160
  8.7 187.0 %all-reduce.11.cloned.1.call-start = ((), (), s32[]{:S(2)}) async-start(), calls=%async_computation.11 | async-start | bytes 4194304 | tf_op jit(solution)/shard_map/psum | solution.py:73
  35.1 79.0 %copy-start.48 = (f32[256]{0:T(256)}, f32[256]{0:T(256)S(1)}, u32[]{:S(2)}) copy-start(f32[256]{0:T(256)S(1)} %get-tuple-element.83) | copy-start | bytes 3076
  69.5 5.6 copy-start.47
  107.8 6.3 copy-start.21
  127.1 2.0 copy-start.3
  127.1 2.0 copy-start.44
  127.7 1.5 copy-start.50
  128.5 2.1 copy-start
  128.5 2.1 copy-start.45
  130.6 40.1 %copy-start.37 = (bf16[64,8,256]{2,0,1:T(8,128)(2,1)}, bf16[64,8,256]{2,0,1:T(8,128)(2,1)S(1)}, u32[]{:S(2)}) copy-start(bf16[64,8,256]{2,0,1:T(8,128)(2,1)S(1)} %fusion.29) | copy-start | bytes 786436
  131.4 44.1 %copy-start.38 = (bf16[64,8,256]{2,0,1:T(8,128)(2,1)}, bf16[64,8,256]{2,0,1:T(8,128)(2,1)S(1)}, u32[]{:S(2)}) copy-start(bf16[64,8,256]{2,0,1:T(8,128)(2,1)S(1)} %fusion.30) | copy-start | bytes 786436
  175.5 1.8 copy-start.60
  175.5 186.5 %all-gather.14.cloned.1.call-start = ((), (), s32[]{:S(2)}) async-start(), calls=%async_computation.13 | async-start | bytes 12976128 | tf_op jit(solution)/shard_map/all_gather | solution.py:170
  176.1 349.5 %all-gather.12.cloned.1.call-start = ((), (), s32[]{:S(2)}) async-start(), calls=%async_computation.12 | async-start | bytes 12976128 | tf_op jit(solution)/shard_map/all_gather | solution.py:169
  176.7 512.5 %all-gather.16.cloned.1.call-start = ((), (), s32[]{:S(2)}) async-start(), calls=%async_computation.14 | async-start | bytes 12976128 | tf_op jit(solution)/shard_map/all_gather | solution.py:176
  177.3 558.6 %all-reduce.13.cloned.1.call-start = ((), (), s32[]{:S(2)}) async-start(), calls=%async_computation.15 | async-start | bytes 4194304 | tf_op jit(solution)/shard_map/psum | solution.py:73
  700.3 7.1 copy-start.25
  700.3 7.1 copy-start.26
  716.2 58.7 %reduce-scatter.12.cloned.1.call-start = ((), (), s32[]{:S(2)}) async-start(), calls=%async_computation.17 | async-start | bytes 393216 | tf_op jit(solution)/shard_map/reduce_scatter | solution.py:241
  735.8 2.9 copy-start.11
  735.8 2.9 copy-start.12
  735.8 2.9 copy-start.55
  735.8 2.9 copy-start.57
  738.7 2.2 copy-start.59
  740.9 3.9 copy-start.42
  744.9 3.8 copy-start.4
  744.9 3.8 copy-start.18
  744.9 3.8 copy-start.28
  744.9 3.8 copy-start.43
  748.7 5.3 copy-start.41
  754.0 3.5 copy-start.1
  754.0 3.5 copy-start.17
  754.0 3.6 copy-start.29
  757.6 3.5 copy-start.36
  761.8 27.7 %reduce-scatter.10.cloned.1.call-start = ((), (), s32[]{:S(2)}) async-start(), calls=%async_computation.16 | async-start | bytes 393216 | tf_op jit(solution)/shard_map/reduce_scatter | solution.py:238
  761.9 4.7 copy-start.2
  761.9 6.7 copy-start.10
  761.9 6.7 copy-start.53
  766.3 3.2 copy-start.7
  769.5 1.5 copy-start.8
  770.3 4.6 copy-start.49
  771.8 89.3 %reduce-scatter.18.cloned.1.call-start = ((), (), s32[]{:S(2)}) async-start(), calls=%async_computation.20 | async-start | bytes 1179648 | tf_op jit(solution)/shard_map/reduce_scatter | solution.py:274
  777.4 147.2 %reduce-scatter.16.cloned.1.call-start = ((), (), s32[]{:S(2)}) async-start(), calls=%async_computation.19 | async-start | bytes 1179648 | tf_op jit(solution)/shard_map/reduce_scatter | solution.py:274
  793.0 281.6 %reduce-scatter.20.cloned.1.call-start = ((), (), s32[]{:S(2)}) async-start(), calls=%async_computation.21 | async-start | bytes 9437184 | tf_op jit(solution)/shard_map/reduce_scatter | solution.py:274
  799.3 425.4 %reduce-scatter.14.cloned.1.call-start = ((), (), s32[]{:S(2)}) async-start(), calls=%async_computation.18 | async-start | bytes 9437184 | tf_op jit(solution)/shard_map/reduce_scatter | solution.py:274
  800.2 2.2 copy-start.9
  809.1 792.1 %reduce-scatter.26.cloned.1.call-start = ((), (), s32[]{:S(2)}) async-start(), calls=%async_computation.24 | async-start | bytes 25952256 | tf_op jit(solution)/shard_map/reduce_scatter | solution.py:274
  821.8 1155.1 %reduce-scatter.24.cloned.1.call-start = ((), (), s32[]{:S(2)}) async-start(), calls=%async_computation.23 | async-start | bytes 25952256 | tf_op jit(solution)/shard_map/reduce_scatter | solution.py:274
  834.5 1518.1 %reduce-scatter.22.cloned.1.call-start = ((), (), s32[]{:S(2)}) async-start(), calls=%async_computation.22 | async-start | bytes 25952256 | tf_op jit(solution)/shard_map/reduce_scatter | solution.py:274
  847.4 1535.7 %all-reduce.15.cloned.1.call-start = ((), (), s32[]{:S(2)}) async-start(), calls=%async_computation.25 | async-start | bytes 8388608 | tf_op jit(solution)/shard_map/psum | solution.py:73
  847.4 9.4 copy-start.24
  847.4 9.4 copy-start.58
  861.0 1780.8 %all-reduce.17.cloned.1.call-start = ((), (), s32[]{:S(2)}) async-start(), calls=%async_computation.26 | async-start | bytes 22020096 | tf_op jit(solution)/shard_map/psum | solution.py:301
  2352.6 32.8 %copy-start.52 = (f32[2048]{0:T(1024)S(1)}, f32[2048]{0:T(1024)}, u32[]{:S(2)}) copy-start(f32[2048]{0:T(1024)} %get-tuple-element.44) | copy-start | bytes 24580
  2352.6 75.9 %copy-start.56 = (f32[256]{0:T(256)S(1)}, f32[256]{0:T(256)}, u32[]{:S(2)}) copy-start(f32[256]{0:T(256)} %get-tuple-element.82) | copy-start | bytes 3076
  2641.9 3.5 copy-start.34
  2645.3 1.7 copy-start.39
  2645.3 2.3 copy-start.33
  2645.3 3.3 copy-start.14
  2648.6 2.9 copy-start.13
  (16 other events, 15.8 us)
Sparse Core Ops, SparseCore 0:
  10.1 86.2 all-gather.7
  98.6 72.0 all-gather.9
  175.6 19.8 all-reduce.10
  197.5 164.4 all-gather.13
  364.1 161.4 all-gather.11
  527.7 161.4 all-gather.15
  716.3 19.4 all-reduce.12
  761.9 12.9 reduce-scatter.11
  777.7 11.7 reduce-scatter.9
  793.3 64.1 reduce-scatter.17
  861.5 63.0 reduce-scatter.15
  928.1 146.3 reduce-scatter.19
  1078.2 146.5 reduce-scatter.13
  1228.5 372.7 reduce-scatter.25
  1605.0 371.8 reduce-scatter.23
  1980.6 371.8 reduce-scatter.21
  2355.5 27.5 all-reduce.14
  2386.0 255.8 all-reduce.16
where the time goes:
time: 2670 us; the launch traced here: 2660 us
  waiting for transfers between devices  2270 us (85%)
  blocking collectives  160 us (6%)
  matrix products  144 us (5%)
  other arithmetic  35.2 us (1%)
  local copies, waits for them, and re-layouts  30.6 us (1%)
    reduce_scatter x7, waiting for transfers between devices, body(): lax.psum_scatter((jnp.sum(grad_normed_one * scaled_one, axis=0), contract...  1490 us
    psum x1, waiting for transfers between devices, body(): lax.psum((gain_one_grad, query_grad, key_grad, value_grad, output_grad, g...  208 us
    all_gather x1, waiting for transfers between devices, body(): lax.all_gather(up_weight, 'fsdp', axis=0, tiled=True)  162 us
    all_gather x1, waiting for transfers between devices, body(): lax.all_gather(down_weight, 'fsdp', axis=0, tiled=True)  154 us
    all_gather x1, waiting for transfers between devices, body(): lax.all_gather(gate_weight, 'fsdp', axis=0, tiled=True)  154 us
  transfers between devices with their start and end apart: 18, of which 15 were waited for; matrix products, arithmetic and copies ran while one was open for 5% of the time, Pallas kernels for 0%

commit v1 on v0

--- a/solution.py
+++ b/solution.py
@@ -2,6 +2,7 @@
 import jax.numpy as jnp
 from jax import lax
 from jax.sharding import PartitionSpec as P
+from jax.lax import all_to_all, psum
 
 HEADS = 32
 KV_HEADS = 4
@@ -172,9 +173,14 @@
     )
     silu_value = gate_lin / (1.0 + jnp.exp(-gate_lin))
     act_low = (silu_value * up_lin).astype(jnp.bfloat16)
-    mlp_branch = tensor_total(
-        column_map(act_low, lax.all_gather(down_weight, "fsdp", axis=0, tiled=True))
-    )
+
+    def manage_marks_all(message, axis_id, in_dim):
+        return jnp.concatenate(
+            all_to_all(jnp.stack(tuple((message for _ in range(psum(1, axis_id))))), axis_id, 0, 0),
+            axis=in_dim,
+        )
+
+    mlp_branch = tensor_total(column_map(act_low, manage_marks_all(down_weight, "fsdp", 0)))
     block_out = (residual + mlp_branch).astype(jnp.bfloat16)
     grad_out = cotangent.astype(jnp.float32)
     grad_act = row_fold(cotangent, lax.all_gather(down_weight, "fsdp", axis=0, tiled=True))

time: 2670 us -> 2810 us (1.052)
  blocking collectives: 160 us -> 540 us
  waiting for transfers between devices: 2270 us -> 2030 us
    all_to_all x0 -> x1, blocking collectives: none -> 379 us  [manage_marks_all(): all_to_all(jnp.stack(tuple((message for _ in range(psum(1, axis_id))))),...]
    reduce_scatter x7, waiting for transfers between devices: 1490 us -> 1250 us  [body(): lax.psum_scatter((jnp.sum(grad_normed_one * scaled_one, axis=0), contract...]
  transfers between devices with their start and end apart: 18 -> 18, of which waited for: 15 -> 13; matrix products, arithmetic and copies ran while one was open for 5% -> 5% of each run, Pallas kernels for 0% -> 0%
where the time goes in v1:
time: 2810 us; the launch traced here: 2800 us
  waiting for transfers between devices  2030 us (72%)
  blocking collectives  540 us (19%)
  matrix products  141 us (5%)
  local copies, waits for them, and re-layouts  36.2 us (1%)
  other arithmetic  35.2 us (1%)
    reduce_scatter x7, waiting for transfers between devices, body(): lax.psum_scatter((jnp.sum(grad_normed_one * scaled_one, axis=0), contract...  1250 us
    all_to_all x1, blocking collectives, manage_marks_all(): all_to_all(jnp.stack(tuple((message for _ in range(psum(1, axis_id))))),...  379 us
    psum x1, waiting for transfers between devices, body(): lax.psum((gain_one_grad, query_grad, key_grad, value_grad, output_grad, g...  208 us
    all_gather x1, waiting for transfers between devices, body(): lax.all_gather(up_weight, 'fsdp', axis=0, tiled=True)  162 us
    all_gather x1, waiting for transfers between devices, body(): lax.all_gather(down_weight, 'fsdp', axis=0, tiled=True)  154 us
    all_gather x1, waiting for transfers between devices, body(): lax.all_gather(gate_weight, 'fsdp', axis=0, tiled=True)  154 us
  transfers between devices with their start and end apart: 18, of which 13 were waited for; matrix products, arithmetic and copies ran while one was open for 5% of the time, Pallas kernels for 0%

profile of v1, /device:TPU:0, one launch (start us, length us, event | category | flops | bytes accessed | tf_op | source)
XLA Modules:
  0.0 2797.2 jit_solution(10149313225332794956)
XLA Ops:
  9.4 22.6 all-gather
  33.0 1.5 fusion.19
  35.1 33.7 %all_gather.42 = bf16[2048,128]{1,0:T(8,128)(2,1)S(1)} all-gather(bf16[256,128]{1,0:T(8,128)(2,1)S(1)} %copy-done.47), channel_id=1, replica_groups=mesh['fsdp'=8,'ctx'=2,'tp'=2] {'fsdp'}, dimensions={0}, use_global_device_ids=true | all-gather | bytes 589824 | tf_op jit(solution)/shard_map/all_gather | solution.py:106
  70.0 5.0 all_gather.43
  75.1 32.7 %all_gather.40 = bf16[2048,128]{1,0:T(8,128)(2,1)S(1)} all-gather(bf16[256,128]{1,0:T(8,128)(2,1)S(1)} %copy-done.48), channel_id=1, replica_groups=mesh['fsdp'=8,'ctx'=2,'tp'=2] {'fsdp'}, dimensions={0}, use_global_device_ids=true | all-gather | bytes 589824 | tf_op jit(solution)/shard_map/all_gather | solution.py:107
  108.3 5.0 all_gather.41
  114.1 3.5 fusion.62
  117.6 1.3 copy.71
  121.3 2.5 copy.72
  123.8 1.4 add_convert_fusion.1
  131.4 39.3 %all-gather.10.cloned.1.call-done = bf16[2048,1024]{1,0:T(8,128)(2,1)} async-done(((bf16[256,1024]{1,0:T(8,128)(2,1)}), bf16[2048,1024]{1,0:T(8,128)(2,1)}) %all-gather.10.cloned.1.call-update) | async-done | bytes 4194320 | tf_op jit(solution)/shard_map/all_gather | solution.py:161
  170.7 4.8 fusion.44
  177.3 18.3 all-gather.1
  195.7 1.9 multiply_reduce_fusion.2
  200.0 162.1 %all-gather.14.cloned.1.call-done = bf16[2048,2816]{1,0:T(8,128)(2,1)} async-done(((bf16[256,2816]{1,0:T(8,128)(2,1)}), bf16[2048,2816]{1,0:T(8,128)(2,1)}) %all-gather.14.cloned.1.call-update) | async-done | bytes 11534352 | tf_op jit(solution)/shard_map/all_gather | solution.py:171
  362.1 9.3 fusion.74
  371.4 154.2 %all-gather.12.cloned.1.call-done = bf16[2048,2816]{1,0:T(8,128)(2,1)} async-done(((bf16[256,2816]{1,0:T(8,128)(2,1)}), bf16[2048,2816]{1,0:T(8,128)(2,1)}) %all-gather.12.cloned.1.call-update) | async-done | bytes 11534352 | tf_op jit(solution)/shard_map/all_gather | solution.py:170
  525.6 9.3 fusion.73
  534.9 154.2 %all-gather.16.cloned.1.call-done = bf16[2048,2816]{1,0:T(8,128)(2,1)} async-done(((bf16[256,2816]{1,0:T(8,128)(2,1)}), bf16[2048,2816]{1,0:T(8,128)(2,1)}) %all-gather.16.cloned.1.call-update) | async-done | bytes 11534352 | tf_op jit(solution)/shard_map/all_gather | solution.py:186
  689.2 11.1 multiply_convert_fusion
  700.3 7.1 fusion.76
  707.4 8.8 convolution_add_fusion.2
  716.2 1.3 log_add_fusion
  717.6 1.3 log_add_fusion.1
  718.9 17.0 all-reduce.13.cloned.1.call-done
  735.8 2.9 multiply_reduce_fusion
  739.3 1.6 copy-done.59
  740.9 1.3 convolution_convert_fusion
  743.1 1.8 copy.82
  744.9 3.8 fusion.34
  748.7 3.5 fusion
  752.2 1.8 copy.79
  754.0 3.1 fusion.31
  757.6 3.4 fusion.3
  761.8 4.4 fusion.2
  766.4 2.0 copy-done.10
  771.7 3.1 reduce-scatter.12.cloned.1.call-done
  774.8 2.5 fusion.51
  777.8 11.6 reduce-scatter.10.cloned.1.call-done
  791.3 1.6 fusion.58
  793.0 2.2 fusion.27
  797.1 4.7 fusion.60
  801.9 6.3 fusion.40
  808.3 12.6 convolution_bitcast_fusion
  821.0 12.6 fusion.79
  833.9 12.6 fusion.78
  846.5 6.4 stack.2
  853.0 379.2 %all_to_all.5 = bf16[8,256,2816]{2,1,0:T(8,128)(2,1)S(1)} all-to-all(bf16[8,256,2816]{2,1,0:T(8,128)(2,1)} %stack.2), channel_id=1, replica_groups=mesh['fsdp'=8,'ctx'=2,'tp'=2] {'fsdp'}, dimensions={0} | all-to-all | bytes 23068672 | tf_op jit(solution)/shard_map/all_to_all | solution.py:179
  1232.2 4.5 fusion.75
  1236.7 3.6 fusion.77
  1241.4 1.8 convolution_add_fusion
  1243.3 118.2 %reduce-scatter.20.cloned.1.call-done = f32[256,1024]{1,0:T(8,128)} async-done(((f32[2048,1024]{1,0:T(8,128)}), f32[256,1024]{1,0:T(8,128)}) %reduce-scatter.20.cloned.1.call-update) | async-done | bytes 1048592 | tf_op jit(solution)/shard_map/reduce_scatter | solution.py:280
  1361.5 376.6 %reduce-scatter.26.cloned.1.call-done = f32[256,2816]{0,1:T(8,128)} async-done(((f32[2048,2816]{0,1:T(8,128)}), f32[256,2816]{0,1:T(8,128)}) %reduce-scatter.26.cloned.1.call-update) | async-done | bytes 2883600 | tf_op jit(solution)/shard_map/reduce_scatter | solution.py:280
  1738.1 375.8 %reduce-scatter.24.cloned.1.call-done = f32[256,2816]{1,0:T(8,128)} async-done(((f32[2048,2816]{1,0:T(8,128)}), f32[256,2816]{1,0:T(8,128)}) %reduce-scatter.24.cloned.1.call-update) | async-done | bytes 2883600 | tf_op jit(solution)/shard_map/reduce_scatter | solution.py:280
  2113.9 375.8 %reduce-scatter.22.cloned.1.call-done = f32[256,2816]{1,0:T(8,128)} async-done(((f32[2048,2816]{1,0:T(8,128)}), f32[256,2816]{1,0:T(8,128)}) %reduce-scatter.22.cloned.1.call-update) | async-done | bytes 2883600 | tf_op jit(solution)/shard_map/reduce_scatter | solution.py:280
  2491.6 28.6 %all-reduce.15.cloned.1.call-done = (f32[256,2048]{1,0:T(8,128)}, f32[256,2048]{1,0:T(8,128)}) async-done(((f32[256,2048]{1,0:T(8,128)}, f32[256,2048]{1,0:T(8,128)}), (f32[256,2048]{1,0:T(8,128)}, f32[256,2048]{1,0:T(8,128)})) %all-reduce.15.cloned.1.call-update) | async-done | bytes 4194320 | tf_op jit(solution)/shard_map/psum | solution.py:74
  2520.2 2.3 fusion.14
  2522.5 37.3 %all-reduce.2 = (f32[2048]{0:T(1024)S(1)}, f32[2048]{0:T(1024)S(1)}) all-reduce(f32[2048]{0:T(1024)S(1)} %get-tuple-element.46, f32[2048]{0:T(1024)S(1)} %copy-done.53), channel_id=4, replica_groups=mesh['fsdp'=8,'ctx'=2,'tp'=2] {'fsdp'}, use_global_device_ids=true, to_apply=%region_17.18.clone | all-reduce | flops 4096 | bytes 32768
  2560.0 5.7 all-reduce.4
  2565.7 5.1 fusion.21
  2570.8 208.2 %all-reduce.17.cloned.1.call-done = (f32[256,1024]{1,0:T(8,128)}, f32[256,128]{1,0:T(8,128)}, f32[256,128]{1,0:T(8,128)}, f32[256,1024]{1,0:T(8,128)}, f32[256,2...) async-done(((f32[256,1024]{1,0:T(8,128)}, f32[256,128]{1,0:T(8,128)}, f32[256,128]{1,0:T(8,128)}, f32[256,1024]{1,0:T(8,128)}, f32[256,2816]{1,0:T(8,128)}, ...) | async-done | bytes 11010064 | tf_op jit(solution)/shard_map/psum | solution.py:307
  2779.0 3.5 copy.89
  2785.8 1.6 copy.121
  2788.6 1.6 copy.122
  (221 shorter events, 36.6 us)
Async XLA Ops:
  7.2 61.7 %copy-start.5 = (bf16[256,2048]{1,0:T(8,128)(2,1)S(1)}, bf16[256,2048]{1,0:T(8,128)(2,1)}, u32[]{:S(2)}) copy-start(bf16[256,2048]{1,0:T(8,128)(2,1)} %param.12) | copy-start | bytes 3145732
  7.2 28.0 copy-start.47
  7.2 106.9 %all-gather.8.cloned.1.call-start = ((), (), s32[]{:S(2)}) async-start(), calls=%async_computation.10 | async-start | bytes 4718592 | tf_op jit(solution)/shard_map/all_gather | solution.py:105
  7.9 162.7 %all-gather.10.cloned.1.call-start = ((), (), s32[]{:S(2)}) async-start(), calls=%async_computation.11 | async-start | bytes 4718592 | tf_op jit(solution)/shard_map/all_gather | solution.py:161
  8.7 187.0 %all-reduce.11.cloned.1.call-start = ((), (), s32[]{:S(2)}) async-start(), calls=%async_computation.12 | async-start | bytes 4194304 | tf_op jit(solution)/shard_map/psum | solution.py:74
  35.1 79.0 %copy-start.49 = (f32[256]{0:T(256)}, f32[256]{0:T(256)S(1)}, u32[]{:S(2)}) copy-start(f32[256]{0:T(256)S(1)} %get-tuple-element.83) | copy-start | bytes 3076
  69.5 5.6 copy-start.48
  107.8 6.3 copy-start.22
  127.1 2.1 copy-start.3
  127.1 2.1 copy-start.45
  128.5 2.0 copy-start
  128.5 2.0 copy-start.46
  130.5 40.2 %copy-start.38 = (bf16[64,8,256]{2,0,1:T(8,128)(2,1)}, bf16[64,8,256]{2,0,1:T(8,128)(2,1)S(1)}, u32[]{:S(2)}) copy-start(bf16[64,8,256]{2,0,1:T(8,128)(2,1)S(1)} %fusion.29) | copy-start | bytes 786436
  131.4 44.1 %copy-start.39 = (bf16[64,8,256]{2,0,1:T(8,128)(2,1)}, bf16[64,8,256]{2,0,1:T(8,128)(2,1)S(1)}, u32[]{:S(2)}) copy-start(bf16[64,8,256]{2,0,1:T(8,128)(2,1)S(1)} %fusion.30) | copy-start | bytes 786436
  175.5 1.8 copy-start.60
  175.5 186.5 %all-gather.14.cloned.1.call-start = ((), (), s32[]{:S(2)}) async-start(), calls=%async_computation.14 | async-start | bytes 12976128 | tf_op jit(solution)/shard_map/all_gather | solution.py:171
  176.1 349.5 %all-gather.12.cloned.1.call-start = ((), (), s32[]{:S(2)}) async-start(), calls=%async_computation.13 | async-start | bytes 12976128 | tf_op jit(solution)/shard_map/all_gather | solution.py:170
  176.7 512.5 %all-gather.16.cloned.1.call-start = ((), (), s32[]{:S(2)}) async-start(), calls=%async_computation.15 | async-start | bytes 12976128 | tf_op jit(solution)/shard_map/all_gather | solution.py:186
  177.3 558.6 %all-reduce.13.cloned.1.call-start = ((), (), s32[]{:S(2)}) async-start(), calls=%async_computation.16 | async-start | bytes 4194304 | tf_op jit(solution)/shard_map/psum | solution.py:74
  700.3 7.1 copy-start.26
  700.3 7.1 copy-start.27
  716.2 58.6 %reduce-scatter.12.cloned.1.call-start = ((), (), s32[]{:S(2)}) async-start(), calls=%async_computation.18 | async-start | bytes 393216 | tf_op jit(solution)/shard_map/reduce_scatter | solution.py:247
  735.8 2.9 copy-start.11
  735.8 2.9 copy-start.12
  735.8 2.9 copy-start.56
  735.8 2.9 copy-start.58
  738.7 2.2 copy-start.59
  740.9 3.9 copy-start.43
  744.9 3.8 copy-start.4
  744.9 3.8 copy-start.19
  744.9 3.8 copy-start.29
  744.9 3.8 copy-start.44
  748.7 5.3 copy-start.42
  754.0 3.5 copy-start.1
  754.0 3.5 copy-start.18
  754.0 3.6 copy-start.30
  757.5 3.4 copy-start.37
  761.7 27.7 reduce-scatter.10.cloned.1.call-start
  761.7 4.7 copy-start.2
  761.8 6.7 copy-start.10
  761.8 6.7 copy-start.54
  766.2 3.2 copy-start.7
  770.2 4.6 copy-start.50
  771.7 471.6 %reduce-scatter.18.cloned.1.call-start = ((), (), s32[]{:S(2)}) async-start(), calls=%async_computation.21 | async-start | bytes 1179648 | tf_op jit(solution)/shard_map/reduce_scatter | solution.py:280
  777.3 466.0 %reduce-scatter.16.cloned.1.call-start = ((), (), s32[]{:S(2)}) async-start(), calls=%async_computation.20 | async-start | bytes 1179648 | tf_op jit(solution)/shard_map/reduce_scatter | solution.py:280
  790.3 2.6 copy-start.32
  792.9 450.4 %reduce-scatter.14.cloned.1.call-start = ((), (), s32[]{:S(2)}) async-start(), calls=%async_computation.19 | async-start | bytes 9437184 | tf_op jit(solution)/shard_map/reduce_scatter | solution.py:280
  793.0 2.2 copy-start.9
  801.8 559.7 %reduce-scatter.20.cloned.1.call-start = ((), (), s32[]{:S(2)}) async-start(), calls=%async_computation.22 | async-start | bytes 9437184 | tf_op jit(solution)/shard_map/reduce_scatter | solution.py:280
  808.2 929.9 %reduce-scatter.26.cloned.1.call-start = ((), (), s32[]{:S(2)}) async-start(), calls=%async_computation.25 | async-start | bytes 25952256 | tf_op jit(solution)/shard_map/reduce_scatter | solution.py:280
  820.9 1293.0 %reduce-scatter.24.cloned.1.call-start = ((), (), s32[]{:S(2)}) async-start(), calls=%async_computation.24 | async-start | bytes 25952256 | tf_op jit(solution)/shard_map/reduce_scatter | solution.py:280
  833.6 1656.1 %reduce-scatter.22.cloned.1.call-start = ((), (), s32[]{:S(2)}) async-start(), calls=%async_computation.23 | async-start | bytes 25952256 | tf_op jit(solution)/shard_map/reduce_scatter | solution.py:280
  846.5 1673.7 %all-reduce.15.cloned.1.call-start = ((), (), s32[]{:S(2)}) async-start(), calls=%async_computation.26 | async-start | bytes 8388608 | tf_op jit(solution)/shard_map/psum | solution.py:74
  853.0 379.2 %copy-start.15 = (bf16[256,2816]{1,0:T(8,128)(2,1)S(1)}, bf16[256,2816]{1,0:T(8,128)(2,1)}, u32[]{:S(2)}) copy-start(bf16[256,2816]{1,0:T(8,128)(2,1)} %get-tuple-element.65) | copy-start | bytes 4325380
  1232.2 4.5 copy-start.25
  1236.7 3.6 copy-start.21
  1243.2 1535.8 %all-reduce.17.cloned.1.call-start = ((), (), s32[]{:S(2)}) async-start(), calls=%async_computation.27 | async-start | bytes 22020096 | tf_op jit(solution)/shard_map/psum | solution.py:307
  2489.7 32.7 %copy-start.53 = (f32[2048]{0:T(1024)S(1)}, f32[2048]{0:T(1024)}, u32[]{:S(2)}) copy-start(f32[2048]{0:T(1024)} %get-tuple-element.44) | copy-start | bytes 24580
  2489.8 75.9 %copy-start.57 = (f32[256]{0:T(256)S(1)}, f32[256]{0:T(256)}, u32[]{:S(2)}) copy-start(f32[256]{0:T(256)} %get-tuple-element.82) | copy-start | bytes 3076
  2779.0 3.5 copy-start.35
  2782.5 1.7 copy-start.40
  2782.5 2.3 copy-start.34
  2782.5 3.3 copy-start.14
  2785.8 2.9 copy-start.13
  (16 other events, 16.5 us)
Sparse Core Ops, SparseCore 0:
  10.1 86.2 all-gather.7
  98.6 72.0 all-gather.9
  175.6 19.8 all-reduce.10
  197.5 164.4 all-gather.13
  364.1 161.4 all-gather.11
  527.7 161.4 all-gather.15
  716.3 19.4 all-reduce.12
  761.8 12.9 reduce-scatter.11
  777.6 11.7 reduce-scatter.9
  793.2 64.1 reduce-scatter.17
  861.4 74.2 reduce-scatter.15
  939.2 268.8 reduce-scatter.13
  1211.7 149.8 reduce-scatter.19
  1365.3 372.7 reduce-scatter.25
  1741.8 372.0 reduce-scatter.23
  2117.6 372.0 reduce-scatter.21
  2492.7 27.5 all-reduce.14
  2523.1 255.8 all-reduce.16
